TPU v7x, 32 devices: a whole 2x2x4 slice. The times are simulated.
32 devices in a mesh: dp: 4 (over z), seq: 8 (over y, x, core).
Axes of the slice: x: 2, y: 2, z: 4, core: 2. Of those that a mesh axis runs over, the one named last changes fastest.
Arguments:
- layer_input: bfloat16 [4, 2048, 1152], P('dp', 'seq'), may hold values from -6 to 6
- segment_ids: int32 [4, 2048], P('dp'), may hold values from 0 to 3, as said below
- position_ids: int32 [4, 2048], P('dp', 'seq'), may hold values from 0 to 1023, as said below
- w_query: bfloat16 [1152, 1024], P('seq'), may hold values from -0.1875 to 0.1875
- w_keyval: bfloat16 [1152, 512], P('seq'), may hold values from -0.1875 to 0.1875
- w_out: bfloat16 [1024, 1152], P('seq'), may hold values from -0.1875 to 0.1875
- w_gate: bfloat16 [1152, 6912], P(None, 'seq'), may hold values from -0.1875 to 0.1875
- w_up: bfloat16 [1152, 6912], P(None, 'seq'), may hold values from -0.1875 to 0.1875
- w_down: bfloat16 [6912, 1152], P('seq'), may hold values from -0.078125 to 0.078125
- g_input: float32 [1152], replicated, may hold values from 0.25 to 1.75
- g_post_attn: float32 [1152], replicated, may hold values from 0.25 to 1.75
- g_pre_ffn: float32 [1152], replicated, may hold values from 0.25 to 1.75
- g_post_ffn: float32 [1152], replicated, may hold values from 0.25 to 1.75
- g_query: float32 [256], replicated, may hold values from 0.25 to 1.75
- g_key: float32 [256], replicated, may hold values from 0.25 to 1.75
- out_grad: float32 [4, 2048, 1152], P('dp', 'seq'), may hold values from -6 to 6
Outputs:
- layer_output: bfloat16 [4, 2048, 1152], P('dp', 'seq')
- input_grad: float32 [4, 2048, 1152], P('dp', 'seq')
- grad_w_query: float32 [1152, 1024], P('seq')
- grad_w_keyval: float32 [1152, 512], P('seq')
- grad_w_out: float32 [1024, 1152], P('seq')
- grad_w_gate: float32 [1152, 6912], P(None, 'seq')
- grad_w_up: float32 [1152, 6912], P(None, 'seq')
- grad_w_down: float32 [6912, 1152], P('seq')
- grad_g_input: float32 [1152], P('seq')
- grad_g_post_attn: float32 [1152], P('seq')
- grad_g_pre_ffn: float32 [1152], P('seq')
- grad_g_post_ffn: float32 [1152], P('seq')
- grad_g_query: float32 [256], P('seq')
- grad_g_key: float32 [256], P('seq')
Inputs may be any that keep to these rules, and one draw needn't show every extreme that they name: `segment_ids`: in each row the ids never fall, start at 0 and rise by one at each document's first token; every row holds 4 documents, none longer than 1024 tokens, and in every row one of them is exactly that long. `position_ids`: A token's place within its document: 0 at the document's first token, rising by one along it; the documents are those of segment_ids.
All inputs are finite; a program needn't handle non-finite values.
Results may differ from a plain program's by a relative error of at most 0.023.
Values may be sent and summed in bfloat16 or wider, within the bound.
No kernel may reach another device: no remote copies, remote signals or barrier semaphores. Data moves between devices by JAX's collectives and lax.ppermute only.
A program may use at most 256 MiB of HBM per device.

v0:
```python
import jax
import jax.numpy as jnp
from jax import lax
from jax.sharding import PartitionSpec as P

HEADS = 4
HEAD = 256
norm_eps = 1e-06
rope_base = 1000000.0


def rms_forward(values):
    factor = lax.rsqrt(jnp.mean(values * values, axis=-1, keepdims=True) + norm_eps)
    return (values * factor, factor)


def rms_backward(upstream, normed, factor):
    return factor * (upstream - normed * jnp.mean(upstream * normed, axis=-1, keepdims=True))


def rope_angles(positions, width):
    half_width = width // 2
    inverse_freq = rope_base ** (-(jnp.arange(half_width).astype(jnp.float32) * 2.0 / width))
    return positions.astype(jnp.float32)[:, None] * inverse_freq[None, :]


def rotate(values, angles):
    half_width = values.shape[-1] // 2
    first_half = values[..., :half_width]
    second_half = values[..., half_width:]
    cosine = jnp.cos(angles)
    sine_part = jnp.sin(angles)
    return jnp.concatenate(
        [
            first_half * cosine - second_half * sine_part,
            second_half * cosine + first_half * sine_part,
        ],
        axis=-1,
    )


def dot_rows(left, right):
    return lax.dot_general(
        left, right, (((1,), (1,)), ((), ())), preferred_element_type=jnp.float32
    )


def dot_cols(left, right):
    return lax.dot_general(
        left, right, (((0,), (0,)), ((), ())), preferred_element_type=jnp.float32
    )


def gelu_gate(gate_proj, up_proj):
    return jax.nn.gelu(gate_proj, approximate=True) * up_proj


def on_device(
    layer_input,
    segment_ids,
    position_ids,
    w_query,
    w_keyval,
    w_out,
    w_gate,
    w_up,
    w_down,
    g_input,
    g_post_attn,
    g_pre_ffn,
    g_post_ffn,
    g_query,
    g_key,
    out_grad,
):
    local_rows = layer_input.shape[1]
    row_len = local_rows * lax.axis_size("seq")
    row_offset = lax.axis_index("seq") * local_rows
    input_f32 = layer_input[0].astype(jnp.float32)
    seg_row = segment_ids[0]
    seg_local = lax.dynamic_slice_in_dim(seg_row, row_offset, local_rows)
    angles = rope_angles(position_ids[0], HEAD)
    score_scale = HEAD ** (-0.5)
    query_full, keyval_full, out_full, gate_full, up_full, down_full = (
        lax.all_gather(w_query, "seq", axis=0, tiled=True),
        lax.all_gather(w_keyval, "seq", axis=0, tiled=True),
        lax.all_gather(w_out, "seq", axis=0, tiled=True),
        lax.all_gather(w_gate, "seq", axis=1, tiled=True),
        lax.all_gather(w_up, "seq", axis=1, tiled=True),
        lax.all_gather(w_down, "seq", axis=0, tiled=True),
    )
    a_normed, a_factor = rms_forward(input_f32)
    a_low = (a_normed * g_input).astype(jnp.bfloat16)
    q_pre = jnp.dot(a_low, query_full, preferred_element_type=jnp.float32).reshape(
        local_rows, HEADS, HEAD
    )
    kv_pre = jnp.dot(a_low, keyval_full, preferred_element_type=jnp.float32)
    q_hat, q_factor = rms_forward(q_pre)
    q_low = rotate(q_hat * g_query, angles[:, None, :]).astype(jnp.bfloat16)
    k_hat, k_factor = rms_forward(kv_pre[:, :HEAD])
    k_low = rotate(k_hat * g_key, angles).astype(jnp.bfloat16)
    kv_low = jnp.concatenate([k_low, kv_pre[:, HEAD:].astype(jnp.bfloat16)], axis=1)
    kv_row = lax.all_gather(kv_low, "seq", axis=0, tiled=True)
    key_block = min(512, row_len)
    first_block = jnp.maximum(row_offset - row_len // 2 + 1, 0) // key_block
    end_block = (row_offset + local_rows - 1) // key_block + 1
    query_rows = q_low.reshape(local_rows * HEADS, HEAD)
    query_index = jnp.broadcast_to(
        (row_offset + jnp.arange(local_rows, dtype=jnp.int32))[:, None], (local_rows, HEADS)
    ).reshape(-1)
    query_seg = jnp.broadcast_to(seg_local[:, None], (local_rows, HEADS)).reshape(-1)

    def block_at(block_num):
        key_start = (block_num * key_block).astype(jnp.int32)
        kv_piece = lax.dynamic_slice_in_dim(kv_row, key_start, key_block, 0)
        seg_piece = lax.dynamic_slice_in_dim(seg_row, key_start, key_block, 0)
        return (key_start, kv_piece, seg_piece)

    def block_scores(key_start, key_rows, key_seg):
        raw_scores = dot_rows(query_rows, key_rows) * score_scale
        key_index = key_start + jnp.arange(key_block, dtype=jnp.int32)
        visible = (key_seg[None, :] == query_seg[:, None]) & (
            key_index[None, :] <= query_index[:, None]
        )
        return (raw_scores, visible)

    def max_and_total(block_num, state_pair):
        row_max, exp_total = state_pair
        key_start, kv_piece, seg_piece = block_at(block_num)
        raw_scores, visible = block_scores(key_start, kv_piece[:, :HEAD], seg_piece)
        masked = jnp.where(visible, raw_scores, -1e30)
        new_max = jnp.maximum(row_max, jnp.max(masked, axis=1))
        shifted = jnp.where(visible, jnp.exp(masked - new_max[:, None]), 0.0)
        exp_total = exp_total * jnp.exp(row_max - new_max) + jnp.sum(shifted, axis=1)
        return (new_max, exp_total)

    start_max = jnp.full((local_rows * HEADS,), -1e30, jnp.float32)
    start_total = jnp.zeros((local_rows * HEADS,), jnp.float32)
    row_max, exp_total = lax.fori_loop(
        first_block, end_block, max_and_total, (start_max, start_total)
    )
    log_total = row_max + jnp.log(exp_total)

    def weighted_sum(block_num, accum):
        key_start, kv_piece, seg_piece = block_at(block_num)
        raw_scores, visible = block_scores(key_start, kv_piece[:, :HEAD], seg_piece)
        attn_prob = jnp.where(visible, jnp.exp(raw_scores - log_total[:, None]), 0.0).astype(
            jnp.bfloat16
        )
        return accum + jnp.dot(attn_prob, kv_piece[:, HEAD:], preferred_element_type=jnp.float32)

    attended_rows = lax.fori_loop(
        first_block, end_block, weighted_sum, jnp.zeros((local_rows * HEADS, HEAD), jnp.float32)
    )
    attended_low = attended_rows.reshape(local_rows, HEADS * HEAD).astype(jnp.bfloat16)
    attn_proj = jnp.dot(attended_low, out_full, preferred_element_type=jnp.float32)
    attn_normed, attn_factor = rms_forward(attn_proj)
    middle = input_f32 + attn_normed * g_post_attn
    b_normed, b_factor = rms_forward(middle)
    b_low = (b_normed * g_pre_ffn).astype(jnp.bfloat16)
    gate_proj = jnp.dot(b_low, gate_full, preferred_element_type=jnp.float32)
    up_proj = jnp.dot(b_low, up_full, preferred_element_type=jnp.float32)
    hidden_low = gelu_gate(gate_proj, up_proj).astype(jnp.bfloat16)
    ffn_out = jnp.dot(hidden_low, down_full, preferred_element_type=jnp.float32)
    ffn_normed, ffn_factor = rms_forward(ffn_out)
    layer_out = (middle + ffn_normed * g_post_ffn).astype(jnp.bfloat16)
    grad_top = out_grad[0]
    gain_post_ffn = jnp.sum(grad_top * ffn_normed, axis=0)
    d_ffn_low = rms_backward(grad_top * g_post_ffn, ffn_normed, ffn_factor).astype(jnp.bfloat16)
    d_hidden = dot_rows(d_ffn_low, down_full)
    grad_down = dot_cols(hidden_low, d_ffn_low)
    _, gelu_back = jax.vjp(gelu_gate, gate_proj, up_proj)
    d_gate, d_up = gelu_back(d_hidden)
    d_gate_low = d_gate.astype(jnp.bfloat16)
    d_up_low = d_up.astype(jnp.bfloat16)
    grad_gate = dot_cols(b_low, d_gate_low)
    grad_upw = dot_cols(b_low, d_up_low)
    d_b = dot_rows(d_gate_low, gate_full) + dot_rows(d_up_low, up_full)
    gain_pre_ffn = jnp.sum(d_b * b_normed, axis=0)
    d_middle = grad_top + rms_backward(d_b * g_pre_ffn, b_normed, b_factor)
    gain_post_attn = jnp.sum(d_middle * attn_normed, axis=0)
    d_attn_low = rms_backward(d_middle * g_post_attn, attn_normed, attn_factor).astype(jnp.bfloat16)
    grad_outw = dot_cols(attended_low, d_attn_low)
    d_attended = dot_rows(d_attn_low, out_full).astype(jnp.bfloat16)
    d_attended_rows = d_attended.reshape(local_rows * HEADS, HEAD)
    row_dot = jnp.sum(d_attended_rows.astype(jnp.float32) * attended_rows, axis=1)

    def attend_back(block_num, carry):
        d_query, d_kv_whole = carry
        key_start, kv_piece, seg_piece = block_at(block_num)
        raw_scores, visible = block_scores(key_start, kv_piece[:, :HEAD], seg_piece)
        attn_prob = jnp.where(visible, jnp.exp(raw_scores - log_total[:, None]), 0.0)
        prob_low = attn_prob.astype(jnp.bfloat16)
        d_prob = dot_rows(d_attended_rows, kv_piece[:, HEAD:])
        d_scores = (attn_prob * (d_prob - row_dot[:, None])).astype(jnp.bfloat16)
        d_query = (
            d_query
            + jnp.dot(d_scores, kv_piece[:, :HEAD], preferred_element_type=jnp.float32)
            * score_scale
        )
        d_keys = dot_cols(d_scores, query_rows) * score_scale
        d_values = dot_cols(prob_low, d_attended_rows)
        d_kv_whole = lax.dynamic_update_slice_in_dim(
            d_kv_whole, jnp.concatenate([d_keys, d_values], axis=1), key_start, 0
        )
        return (d_query, d_kv_whole)

    d_query, d_kv_whole = lax.fori_loop(
        first_block,
        end_block,
        attend_back,
        (
            jnp.zeros((local_rows * HEADS, HEAD), jnp.float32),
            jnp.zeros((row_len, 2 * HEAD), jnp.float32),
        ),
    )
    d_kv = lax.psum_scatter(
        d_kv_whole.astype(jnp.bfloat16), "seq", scatter_dimension=0, tiled=True
    ).astype(jnp.float32)
    d_q_normed = rotate(d_query.reshape(local_rows, HEADS, HEAD), -angles[:, None, :])
    gain_query = jnp.sum(d_q_normed * q_hat, axis=(0, 1))
    d_q_pre = (
        rms_backward(d_q_normed * g_query, q_hat, q_factor)
        .reshape(local_rows, HEADS * HEAD)
        .astype(jnp.bfloat16)
    )
    d_k_normed = rotate(d_kv[:, :HEAD], -angles)
    gain_key = jnp.sum(d_k_normed * k_hat, axis=0)
    d_k_pre = rms_backward(d_k_normed * g_key, k_hat, k_factor)
    d_kv_low = jnp.concatenate([d_k_pre, d_kv[:, HEAD:]], axis=1).astype(jnp.bfloat16)
    grad_queryw = dot_cols(a_low, d_q_pre)
    grad_keyvalw = dot_cols(a_low, d_kv_low)
    d_a = dot_rows(d_q_pre, query_full) + dot_rows(d_kv_low, keyval_full)
    gain_input = jnp.sum(d_a * a_normed, axis=0)
    d_input = d_middle + rms_backward(d_a * g_input, a_normed, a_factor)
    (
        grad_queryw,
        grad_keyvalw,
        grad_outw,
        grad_gate,
        grad_upw,
        grad_down,
        gain_input,
        gain_post_attn,
        gain_pre_ffn,
        gain_post_ffn,
        gain_query,
        gain_key,
    ) = (
        lax.psum_scatter(
            grad_queryw.astype(jnp.bfloat16), "seq", scatter_dimension=0, tiled=True
        ).astype(jnp.float32),
        lax.psum_scatter(
            grad_keyvalw.astype(jnp.bfloat16), "seq", scatter_dimension=0, tiled=True
        ).astype(jnp.float32),
        lax.psum_scatter(
            grad_outw.astype(jnp.bfloat16), "seq", scatter_dimension=0, tiled=True
        ).astype(jnp.float32),
        lax.psum_scatter(
            grad_gate.astype(jnp.bfloat16), "seq", scatter_dimension=1, tiled=True
        ).astype(jnp.float32),
        lax.psum_scatter(
            grad_upw.astype(jnp.bfloat16), "seq", scatter_dimension=1, tiled=True
        ).astype(jnp.float32),
        lax.psum_scatter(
            grad_down.astype(jnp.bfloat16), "seq", scatter_dimension=0, tiled=True
        ).astype(jnp.float32),
        lax.psum_scatter(
            gain_input.astype(jnp.bfloat16), "seq", scatter_dimension=0, tiled=True
        ).astype(jnp.float32),
        lax.psum_scatter(
            gain_post_attn.astype(jnp.bfloat16), "seq", scatter_dimension=0, tiled=True
        ).astype(jnp.float32),
        lax.psum_scatter(
            gain_pre_ffn.astype(jnp.bfloat16), "seq", scatter_dimension=0, tiled=True
        ).astype(jnp.float32),
        lax.psum_scatter(
            gain_post_ffn.astype(jnp.bfloat16), "seq", scatter_dimension=0, tiled=True
        ).astype(jnp.float32),
        lax.psum_scatter(
            gain_query.astype(jnp.bfloat16), "seq", scatter_dimension=0, tiled=True
        ).astype(jnp.float32),
        lax.psum_scatter(
            gain_key.astype(jnp.bfloat16), "seq", scatter_dimension=0, tiled=True
        ).astype(jnp.float32),
    )
    totals = (
        lax.psum(grad_queryw.astype(jnp.bfloat16), "dp").astype(jnp.float32),
        lax.psum(grad_keyvalw.astype(jnp.bfloat16), "dp").astype(jnp.float32),
        lax.psum(grad_outw.astype(jnp.bfloat16), "dp").astype(jnp.float32),
        lax.psum(grad_gate.astype(jnp.bfloat16), "dp").astype(jnp.float32),
        lax.psum(grad_upw.astype(jnp.bfloat16), "dp").astype(jnp.float32),
        lax.psum(grad_down.astype(jnp.bfloat16), "dp").astype(jnp.float32),
        lax.psum(gain_input.astype(jnp.bfloat16), "dp").astype(jnp.float32),
        lax.psum(gain_post_attn.astype(jnp.bfloat16), "dp").astype(jnp.float32),
        lax.psum(gain_pre_ffn.astype(jnp.bfloat16), "dp").astype(jnp.float32),
        lax.psum(gain_post_ffn.astype(jnp.bfloat16), "dp").astype(jnp.float32),
        lax.psum(gain_query.astype(jnp.bfloat16), "dp").astype(jnp.float32),
        lax.psum(gain_key.astype(jnp.bfloat16), "dp").astype(jnp.float32),
    )
    return (
        layer_out[None],
        d_input[None],
        totals[0],
        totals[1],
        totals[2],
        totals[3],
        totals[4],
        totals[5],
        totals[6],
        totals[7],
        totals[8],
        totals[9],
        totals[10],
        totals[11],
    )


def solution(mesh):
    in_specs = (
        P("dp", "seq", None),
        P("dp", None),
        P("dp", "seq"),
        P("seq", None),
        P("seq", None),
        P("seq", None),
        P(None, "seq"),
        P(None, "seq"),
        P("seq", None),
        P(),
        P(),
        P(),
        P(),
        P(),
        P(),
        P("dp", "seq", None),
    )
    out_specs = (
        P("dp", "seq", None),
        P("dp", "seq", None),
        P("seq", None),
        P("seq", None),
        P("seq", None),
        P(None, "seq"),
        P(None, "seq"),
        P("seq", None),
        P("seq"),
        P("seq"),
        P("seq"),
        P("seq"),
        P("seq"),
        P("seq"),
    )
    return jax.shard_map(
        on_device, mesh=mesh, in_specs=in_specs, out_specs=out_specs, check_vma=False
    )
```

profile of v0, /device:TPU:0, one launch (start us, length us, event | category | flops | bytes accessed | tf_op | source)
XLA Modules:
  0.0 1255.0 jit_solution(4688408701022514957)
XLA Ops:
  9.4 1.3 fusion.63
  10.7 26.0 %all-gather.8.cloned.1.call-done = bf16[1152,512]{1,0:T(8,128)(2,1)} async-done(((bf16[144,512]{1,0:T(8,128)(2,1)}), bf16[1152,512]{1,0:T(8,128)(2,1)}) %all-gather.8.cloned.1.call-update) | async-done | bytes 1179664 | tf_op jit(solution)/shard_map/all_gather | solution.py:86
  36.7 2.0 fusion.78
  39.7 1.8 fusion.72
  41.5 0.7 pad_maximum_fusion.3
  44.8 22.8 %all-gather.12.cloned.1.call-done = bf16[1152,1024]{1,0:T(8,128)(2,1)} async-done(((bf16[144,1024]{1,0:T(8,128)(2,1)}), bf16[1152,1024]{1,0:T(8,128)(2,1)}) %all-gather.12.cloned.1.call-update) | async-done | bytes 2359312 | tf_op jit(solution)/shard_map/all_gather | solution.py:85
  67.6 3.1 copy.39
  70.8 1.0 multiply_reduce_fusion.11
  73.0 25.0 %all-gather.10.cloned.1.call-done = bf16[2048,512]{1,0:T(8,128)(2,1)} async-done(((bf16[256,512]{1,0:T(8,128)(2,1)}), bf16[2048,512]{1,0:T(8,128)(2,1)}) %all-gather.10.cloned.1.call-update) | async-done | bytes 2097168 | tf_op jit(solution)/shard_map/all_gather | solution.py:103
  98.0 2.9 while.37
  98.6 1.6 fusion.144
  100.2 0.7 select_reduce_fusion.2
  101.0 2.8 while.38
  101.6 2.2 fusion.148
  104.8 24.0 %all-gather.14.cloned.1.call-done = bf16[1024,1152]{1,0:T(8,128)(2,1)} async-done(((bf16[128,1152]{1,0:T(8,128)(2,1)}), bf16[1024,1152]{1,0:T(8,128)(2,1)}) %all-gather.14.cloned.1.call-update) | async-done | bytes 2359312 | tf_op jit(solution)/shard_map/all_gather | solution.py:87
  128.8 2.7 multiply_reduce_fusion.7
  132.4 84.5 %all-gather.16.cloned.1.call-done = bf16[1152,6912]{0,1:T(8,128)(2,1)} async-done(((bf16[1152,864]{0,1:T(8,128)(2,1)}), bf16[1152,6912]{0,1:T(8,128)(2,1)}) %all-gather.16.cloned.1.call-update) | async-done | bytes 15925264 | tf_op jit(solution)/shard_map/all_gather | solution.py:88
  216.9 16.5 %fusion.84 = f32[256,6912]{1,0:T(8,128)} fusion(bf16[256,1152]{1,0:T(8,128)(2,1)S(1)} %multiply_convert_fusion.4, bf16[1152,6912]{0,1:T(8,128)(2,1)} %all-gather.16.cloned.1.call-done), kind=kOutput, calls=%fused_computation.160 | convolution fusion | flops 4076863488 | bytes 23592960 | tf_op jit(solution)/shard_map/dot_general | solution.py:161
  233.4 71.5 %all-gather.18.cloned.1.call-done = bf16[1152,6912]{0,1:T(8,128)(2,1)} async-done(((bf16[1152,864]{0,1:T(8,128)(2,1)}), bf16[1152,6912]{0,1:T(8,128)(2,1)}) %all-gather.18.cloned.1.call-update) | async-done | bytes 15925264 | tf_op jit(solution)/shard_map/all_gather | solution.py:89
  304.9 12.7 %multiply_convert_fusion.1 = (bf16[256,6912]{1,0:T(8,128)(2,1)}, f32[256,6912]{1,0:T(8,128)}) fusion(f32[256,6912]{1,0:T(8,128)} %fusion.84, bf16[256,1152]{1,0:T(8,128)(2,1)S(1)} %multiply_convert_fusion.4, bf16[1152,6912]{0,1:T(8,128)(2,1)} %all-gather.18.cloned.1.call-done), kind=kOutput, calls=%fused_computation.61 | convolution fusion | flops 4094558208 | bytes 34209792 | tf_op jit(solution)/shard_map/dot_general | solution.py:162
  317.6 75.5 %all-gather.20.cloned.1.call-done = bf16[6912,1152]{1,0:T(8,128)(2,1)} async-done(((bf16[864,1152]{1,0:T(8,128)(2,1)}), bf16[6912,1152]{1,0:T(8,128)(2,1)}) %all-gather.20.cloned.1.call-update) | async-done | bytes 15925264 | tf_op jit(solution)/shard_map/all_gather | solution.py:90
  393.1 10.5 multiply_reduce_fusion.5
  404.0 1.2 multiply_convert_fusion.3
  405.2 16.0 %multiply_convert_fusion = (bf16[256,6912]{1,0:T(8,128)(2,1)}, bf16[256,6912]{1,0:T(8,128)(2,1)}) fusion(f32[256,6912]{1,0:T(8,128)} %fusion.84, f32[256,6912]{1,0:T(8,128)} %get-tuple-element.378, bf16[256,1152]{1,0:T(8,128)(2,1)S(1)} %get-tuple-element.359, bf16[6912,1152]{1,0:T(8,128)(2,1)} %all-gather.20.cloned.1.call-done), kind=kOutput, calls=%fused_computation.60 | convolution fusion | flops 4119330816 | bytes 37748736 | tf_op jit(solution)/shard_map/dot_general | solution.py:43
  421.3 10.5 fusion.85
  431.8 9.5 multiply_reduce_fusion
  441.3 0.8 multiply_reduce_fusion.1
  443.1 0.8 copy-done.24
  444.4 0.9 convolution_convert_fusion.6
  445.8 1.1 broadcast.270
  446.9 1.5 broadcast_in_dim.41.clone
  448.4 7.5 while.39
  448.9 1.7 bitcast_select_fusion.4
  450.6 1.5 fusion.159
  452.2 1.6 fusion.160
  455.1 0.8 constant_dynamic-update-slice_fusion.2
  456.2 0.9 copy-done.2
  460.2 2.3 convolution_convert_fusion.4
  462.7 2.3 convolution_convert_fusion.3
  465.0 47.4 %reduce-scatter.8.cloned.1.call-done = bf16[256,512]{1,0:T(8,128)(2,1)} async-done(((bf16[2048,512]{1,0:T(8,128)(2,1)}), bf16[256,512]{1,0:T(8,128)(2,1)}) %reduce-scatter.8.cloned.1.call-update) | async-done | bytes 262160 | tf_op jit(solution)/shard_map/reduce_scatter | solution.py:217
  512.4 0.9 slice.80
  513.3 1.0 convert_element_type.215
  515.3 1.6 convolution_convert_fusion.5
  517.0 10.9 convolution_convert_fusion.2
  528.0 11.0 convolution_convert_fusion.1
  539.1 1.0 copy-done.22
  540.1 10.9 convolution_convert_fusion
  551.3 7.4 reduce-scatter.10.cloned.1.call-done
  558.7 45.7 %reduce-scatter.14.cloned.1.call-done = bf16[128,1152]{1,0:T(8,128)(2,1)} async-done(((bf16[1024,1152]{1,0:T(8,128)(2,1)}), bf16[128,1152]{1,0:T(8,128)(2,1)}) %reduce-scatter.14.cloned.1.call-update) | async-done | bytes 294928 | tf_op jit(solution)/shard_map/reduce_scatter | solution.py:256
  604.4 40.4 %reduce-scatter.12.cloned.1.call-done = bf16[144,512]{1,0:T(8,128)(2,1)} async-done(((bf16[1152,512]{1,0:T(8,128)(2,1)}), bf16[144,512]{1,0:T(8,128)(2,1)}) %reduce-scatter.12.cloned.1.call-update) | async-done | bytes 147472 | tf_op jit(solution)/shard_map/reduce_scatter | solution.py:253
  644.8 116.4 %reduce-scatter.16.cloned.1.call-done = bf16[1152,864]{0,1:T(8,128)(2,1)} async-done(((bf16[1152,6912]{0,1:T(8,128)(2,1)}), bf16[1152,864]{0,1:T(8,128)(2,1)}) %reduce-scatter.16.cloned.1.call-update) | async-done | bytes 1990672 | tf_op jit(solution)/shard_map/reduce_scatter | solution.py:259
  761.1 117.0 %reduce-scatter.18.cloned.1.call-done = bf16[1152,864]{0,1:T(8,128)(2,1)} async-done(((bf16[1152,6912]{0,1:T(8,128)(2,1)}), bf16[1152,864]{0,1:T(8,128)(2,1)}) %reduce-scatter.18.cloned.1.call-update) | async-done | bytes 1990672 | tf_op jit(solution)/shard_map/reduce_scatter | solution.py:262
  878.1 116.4 %reduce-scatter.20.cloned.1.call-done = bf16[864,1152]{1,0:T(8,128)(2,1)} async-done(((bf16[6912,1152]{1,0:T(8,128)(2,1)}), bf16[864,1152]{1,0:T(8,128)(2,1)}) %reduce-scatter.20.cloned.1.call-update) | async-done | bytes 1990672 | tf_op jit(solution)/shard_map/reduce_scatter | solution.py:265
  997.6 2.9 fusion.62
  1000.5 24.3 %all-reduce.6 = (bf16[1152]{0:T(1024)(128)(2,1)S(1)}, bf16[1152]{0:T(1024)(128)(2,1)S(1)}, bf16[1152]{0:T(1024)(128)(2,1)S(1)}, bf16[1152]{0:T(1024)(128)(2,1)S(...) all-reduce(bf16[1152]{0:T(1024)(128)(2,1)S(1)} %get-tuple-element.2, ...), channel_id=9, replica_groups=mesh['dp'=4,'seq'=8] {'seq'}, use_global_device_ids=true, to_apply=%region_35.36.clone | all-reduce | flops 5120 | bytes 20480
  1025.2 12.4 all-reduce.7
  1040.9 1.3 fusion.61
  1042.3 193.6 %all-reduce.11.cloned.1.call-done = (bf16[144,1024]{1,0:T(8,128)(2,1)}, bf16[144,512]{1,0:T(8,128)(2,1)}, bf16[128,1152]{1,0:T(8,128)(2,1)}, bf16[1152,864]{0,1:...) async-done(((bf16[144,1024]{1,0:T(8,128)(2,1)}, bf16[144,512]{1,0:T(8,128)(2,1)}, bf16[128,1152]{1,0:T(8,128)(2,1)}, bf16[1152,864]{0,1:T(8,128)(2,1)}, ...) | async-done | bytes 6709264 | tf_op jit(solution)/shard_map/psum | solution.py:288
  1235.8 2.0 convert_element_type.217
  1237.8 1.7 convert_element_type.219
  1239.5 1.8 convert_element_type.221
  1241.3 2.2 convert_element_type.223
  1243.7 2.2 convert_element_type.225
  1246.0 2.2 convert_element_type.227
  (211 shorter events, 24.6 us)
Async XLA Ops:
  7.2 32.4 %copy-start.43 = (f32[256]{0:T(256)S(1)}, f32[256]{0:T(256)}, u32[]{:S(2)}) copy-start(f32[256]{0:T(256)} %param.36) | copy-start | bytes 3076
  7.2 29.5 %all-gather.8.cloned.1.call-start = ((), (), s32[]{:S(2)}) async-start(), calls=%async_computation.7 | async-start | bytes 1327104 | tf_op jit(solution)/shard_map/all_gather | solution.py:86
  7.9 59.7 %all-gather.12.cloned.1.call-start = ((), (), s32[]{:S(2)}) async-start(), calls=%async_computation.9 | async-start | bytes 2654208 | tf_op jit(solution)/shard_map/all_gather | solution.py:85
  8.7 89.4 %all-gather.10.cloned.1.call-start = ((), (), s32[]{:S(2)}) async-start(), calls=%async_computation.8 | async-start | bytes 2359296 | tf_op jit(solution)/shard_map/all_gather | solution.py:103
  9.4 30.3 %copy-start.45 = (f32[1,256]{1,0:T(1,128)}, f32[1,256]{1,0:T(1,128)S(1)}, u32[]{:S(2)}) copy-start(f32[1,256]{1,0:T(1,128)S(1)} %convert_element_type.195) | copy-start | bytes 3076
  9.4 32.1 %copy-start.47 = (f32[128]{0:T(128)}, f32[128]{0:T(128)S(1)}, u32[]{:S(2)}) copy-start(f32[128]{0:T(128)S(1)} %negate_power_fusion) | copy-start | bytes 1540
  10.7 60.0 %copy-start.38 = (f32[256]{0:T(256)}, f32[256]{0:T(256)S(1)}, u32[]{:S(2)}) copy-start(f32[256]{0:T(256)S(1)} %add_rsqrt_fusion.5) | copy-start | bytes 3076
  38.7 0.8 copy-start.19
  39.6 1.9 copy-start.40
  42.2 86.6 %all-gather.14.cloned.1.call-start = ((), (), s32[]{:S(2)}) async-start(), calls=%async_computation.10 | async-start | bytes 2654208 | tf_op jit(solution)/shard_map/all_gather | solution.py:87
  42.8 174.0 %all-gather.16.cloned.1.call-start = ((), (), s32[]{:S(2)}) async-start(), calls=%async_computation.11 | async-start | bytes 17915904 | tf_op jit(solution)/shard_map/all_gather | solution.py:88
  43.4 1.4 copy-start.32
  43.4 261.5 %all-gather.18.cloned.1.call-start = ((), (), s32[]{:S(2)}) async-start(), calls=%async_computation.12 | async-start | bytes 17915904 | tf_op jit(solution)/shard_map/all_gather | solution.py:89
  44.0 349.1 %all-gather.20.cloned.1.call-start = ((), (), s32[]{:S(2)}) async-start(), calls=%async_computation.13 | async-start | bytes 17915904 | tf_op jit(solution)/shard_map/all_gather | solution.py:90
  44.7 467.7 %reduce-scatter.8.cloned.1.call-start = ((), (), s32[]{:S(2)}) async-start(), calls=%async_computation.14 | async-start | bytes 2359296 | tf_op jit(solution)/shard_map/reduce_scatter | solution.py:217
  67.6 3.1 copy-start.3
  67.6 3.1 copy-start.34
  70.7 1.0 copy-start.42
  71.8 1.0 copy-start.10
  103.9 1.0 copy-start.12
  104.8 26.7 %copy-start.16 = (bf16[256,1024]{1,0:T(8,128)(2,1)}, bf16[256,1024]{1,0:T(8,128)(2,1)S(1)}, u32[]{:S(2)}) copy-start(bf16[256,1024]{1,0:T(8,128)(2,1)S(1)} %convert_element_type.202) | copy-start | bytes 1572868
  104.8 26.7 %copy-start.33 = (f32[1152]{0:T(1024)S(1)}, f32[1152]{0:T(1024)}, u32[]{:S(2)}) copy-start(f32[1152]{0:T(1024)} %param.32) | copy-start | bytes 13828
  128.8 2.7 copy-start.4
  131.5 0.7 copy-start.37
  132.4 172.5 %copy-start.14 = (bf16[256,1152]{1,0:T(8,128)(2,1)}, bf16[256,1152]{1,0:T(8,128)(2,1)S(1)}, u32[]{:S(2)}) copy-start(bf16[256,1152]{1,0:T(8,128)(2,1)S(1)} %multiply_convert_fusion.4) | copy-start | bytes 1769476
  393.1 10.5 copy-start.8
  393.1 10.5 copy-start.36
  405.2 16.0 %copy-start.21 = (bf16[256,1152]{1,0:T(8,128)(2,1)}, bf16[256,1152]{1,0:T(8,128)(2,1)S(1)}, u32[]{:S(2)}) copy-start(bf16[256,1152]{1,0:T(8,128)(2,1)S(1)} %get-tuple-element.359) | copy-start | bytes 1769476
  421.3 10.5 copy-start.18
  431.8 9.5 copy-start.9
  442.1 1.0 copy-start.6
  442.1 2.3 copy-start.23
  443.1 0.8 copy-start.24
  444.4 1.2 copy-start.13
  450.6 1.5 copy-start
  453.8 1.0 copy-start.1
  455.9 1.2 copy-start.2
  455.9 102.7 %reduce-scatter.10.cloned.1.call-start = ((), (), s32[]{:S(2)}) async-start(), calls=%async_computation.15 | async-start | bytes 2654208 | tf_op jit(solution)/shard_map/reduce_scatter | solution.py:250
  457.1 0.9 copy-start.30
  457.1 1.0 copy-start.31
  457.4 1.3 copy-start.11
  459.2 1.1 copy-start.5
  459.2 1.1 copy-start.35
  459.2 1.1 copy-start.39
  460.2 2.4 copy-start.17
  460.2 2.4 copy-start.25
  462.6 141.8 %reduce-scatter.14.cloned.1.call-start = ((), (), s32[]{:S(2)}) async-start(), calls=%async_computation.17 | async-start | bytes 2654208 | tf_op jit(solution)/shard_map/reduce_scatter | solution.py:256
  464.9 49.4 %copy-start.46 = (f32[1,256]{1,0:T(1,128)S(1)}, f32[1,256]{1,0:T(1,128)}, u32[]{:S(2)}) copy-start(f32[1,256]{1,0:T(1,128)} %copy-done.45) | copy-start | bytes 3076
  464.9 49.4 %copy-start.48 = (f32[128]{0:T(128)S(1)}, f32[128]{0:T(128)}, u32[]{:S(2)}) copy-start(f32[128]{0:T(128)} %copy-done.47) | copy-start | bytes 1540
  464.9 50.0 %copy-start.20 = (f32[256,512]{1,0:T(8,128)S(1)}, f32[256,512]{1,0:T(8,128)}, u32[]{:S(2)}) copy-start(f32[256,512]{1,0:T(8,128)} %copy-done.19) | copy-start | bytes 1572868
  464.9 50.0 %copy-start.41 = (f32[256]{0:T(256)S(1)}, f32[256]{0:T(256)}, u32[]{:S(2)}) copy-start(f32[256]{0:T(256)} %copy-done.40) | copy-start | bytes 3076
  465.0 50.0 %copy-start.44 = (f32[256]{0:T(256)S(1)}, f32[256]{0:T(256)}, u32[]{:S(2)}) copy-start(f32[256]{0:T(256)} %param.36) | copy-start | bytes 3076
  465.0 179.8 %reduce-scatter.12.cloned.1.call-start = ((), (), s32[]{:S(2)}) async-start(), calls=%async_computation.16 | async-start | bytes 1327104 | tf_op jit(solution)/shard_map/reduce_scatter | solution.py:253
  515.2 1.9 copy-start.15
  517.0 244.2 %reduce-scatter.16.cloned.1.call-start = ((), (), s32[]{:S(2)}) async-start(), calls=%async_computation.18 | async-start | bytes 17915904 | tf_op jit(solution)/shard_map/reduce_scatter | solution.py:259
  528.0 350.1 %reduce-scatter.18.cloned.1.call-start = ((), (), s32[]{:S(2)}) async-start(), calls=%async_computation.19 | async-start | bytes 17915904 | tf_op jit(solution)/shard_map/reduce_scatter | solution.py:262
  539.0 1.1 copy-start.22
  539.0 455.4 %reduce-scatter.20.cloned.1.call-start = ((), (), s32[]{:S(2)}) async-start(), calls=%async_computation.20 | async-start | bytes 17915904 | tf_op jit(solution)/shard_map/reduce_scatter | solution.py:265
  551.0 684.9 %all-reduce.11.cloned.1.call-start = ((), (), s32[]{:S(2)}) async-start(), calls=%async_computation.21 | async-start | bytes 13418496 | tf_op jit(solution)/shard_map/psum | solution.py:288
  994.5 2.5 copy-start.29
  997.5 43.4 %copy-start.7 = (f32[256,1152]{1,0:T(8,128)S(1)}, f32[256,1152]{1,0:T(8,128)}, u32[]{:S(2)}) copy-start(f32[256,1152]{1,0:T(8,128)} %copy-done.6) | copy-start | bytes 3538948
  1235.8 5.4 copy-start.28
  1241.3 2.4 copy-start.27
  1243.7 2.4 copy-start.26
  (1 other events, 0.7 us)
Sparse Core Ops, SparseCore 0:
  9.9 26.7 all-gather.7
  38.6 29.0 all-gather.11
  70.1 27.8 all-gather.9
  99.8 29.0 all-gather.13
  130.6 86.2 all-gather.15
  218.6 86.2 all-gather.17
  306.8 86.2 all-gather.19
  456.1 56.3 reduce-scatter.7
  516.1 42.4 reduce-scatter.9
  561.9 42.4 reduce-scatter.13
  607.9 36.7 reduce-scatter.11
  648.2 112.8 reduce-scatter.15
  765.2 112.8 reduce-scatter.17
  881.6 112.8 reduce-scatter.19
  997.4 238.3 all-reduce.10
where the time goes:
time: 1260 us
  waiting for transfers between devices  1020 us (81%)
  matrix products  134 us (11%)
  blocking collectives  36.7 us (3%)
  other arithmetic  28.9 us (2%)
  local copies, waits for them, and re-layouts  20.3 us (2%)
  between operations  16.2 us (1%)
    psum x1, waiting for transfers between devices, on_device(): lax.psum(grad_queryw.astype(jnp.bfloat16), 'dp').astype(jnp.float32)  194 us
    reduce_scatter x1, waiting for transfers between devices, on_device(): lax.psum_scatter(grad_upw.astype(jnp.bfloat16), 'seq', scatter_dimension=...  117 us
    reduce_scatter x1, waiting for transfers between devices, on_device(): lax.psum_scatter(grad_down.astype(jnp.bfloat16), 'seq', scatter_dimension...  116 us
    reduce_scatter x1, waiting for transfers between devices, on_device(): lax.psum_scatter(grad_gate.astype(jnp.bfloat16), 'seq', scatter_dimension...  116 us
    all_gather x1, waiting for transfers between devices, on_device(): lax.all_gather(w_gate, 'seq', axis=1, tiled=True)  84.5 us
    all_gather x1, waiting for transfers between devices, on_device(): lax.all_gather(w_down, 'seq', axis=0, tiled=True)  75.5 us
    all_gather x1, waiting for transfers between devices, on_device(): lax.all_gather(w_up, 'seq', axis=1, tiled=True)  71.5 us
    reduce_scatter x1, waiting for transfers between devices, on_device(): lax.psum_scatter(d_kv_whole.astype(jnp.bfloat16), 'seq', scatter_dimensio...  47.4 us
  transfers between devices with their start and end apart: 15, of which 15 were waited for; matrix products, arithmetic and copies ran while one was open for 8% of the time, Pallas kernels for 0%

commit v1 on v0

--- a/solution.py
+++ b/solution.py
@@ -7,6 +7,12 @@
 HEAD = 256
 norm_eps = 1e-06
 rope_base = 1000000.0
+
+
+def gather_and_add(x, axis):
+    terms = lax.all_gather(x, axis, axis=0, tiled=False)
+    total = terms.sum(axis=0)
+    return total
 
 
 def rms_forward(values):
@@ -285,7 +291,7 @@
         ).astype(jnp.float32),
     )
     totals = (
-        lax.psum(grad_queryw.astype(jnp.bfloat16), "dp").astype(jnp.float32),
+        gather_and_add(grad_queryw.astype(jnp.bfloat16), "dp").astype(jnp.float32),
         lax.psum(grad_keyvalw.astype(jnp.bfloat16), "dp").astype(jnp.float32),
         lax.psum(grad_outw.astype(jnp.bfloat16), "dp").astype(jnp.float32),
         lax.psum(grad_gate.astype(jnp.bfloat16), "dp").astype(jnp.float32),

time: 1260 us -> 1280 us (1.016)
  waiting for transfers between devices: 1020 us -> 1040 us
    psum x1, waiting for transfers between devices: 194 us -> 213 us  [on_device(): lax.psum(grad_keyvalw.astype(jnp.bfloat16), 'dp').astype(jnp.float32)]
  transfers between devices with their start and end apart: 15 -> 16, of which waited for: 15 -> 15; matrix products, arithmetic and copies ran while one was open for 8% -> 8% of each run, Pallas kernels for 0% -> 0%
where the time goes in v1:
time: 1280 us
  waiting for transfers between devices  1040 us (81%)
  matrix products  134 us (10%)
  blocking collectives  36.1 us (3%)
  other arithmetic  31 us (2%)
  local copies, waits for them, and re-layouts  20.1 us (2%)
  between operations  16.3 us (1%)
    psum x1, waiting for transfers between devices, on_device(): lax.psum(grad_keyvalw.astype(jnp.bfloat16), 'dp').astype(jnp.float32)  213 us
    reduce_scatter x1, waiting for transfers between devices, on_device(): lax.psum_scatter(grad_upw.astype(jnp.bfloat16), 'seq', scatter_dimension=...  117 us
    reduce_scatter x1, waiting for transfers between devices, on_device(): lax.psum_scatter(grad_gate.astype(jnp.bfloat16), 'seq', scatter_dimension...  116 us
    reduce_scatter x1, waiting for transfers between devices, on_device(): lax.psum_scatter(grad_down.astype(jnp.bfloat16), 'seq', scatter_dimension...  116 us
    all_gather x1, waiting for transfers between devices, on_device(): lax.all_gather(w_gate, 'seq', axis=1, tiled=True)  84.5 us
    all_gather x1, waiting for transfers between devices, on_device(): lax.all_gather(w_down, 'seq', axis=0, tiled=True)  75.5 us
    all_gather x1, waiting for transfers between devices, on_device(): lax.all_gather(w_up, 'seq', axis=1, tiled=True)  71.5 us
    reduce_scatter x1, waiting for transfers between devices, on_device(): lax.psum_scatter(d_kv_whole.astype(jnp.bfloat16), 'seq', scatter_dimensio...  47.4 us
  transfers between devices with their start and end apart: 16, of which 15 were waited for; matrix products, arithmetic and copies ran while one was open for 8% of the time, Pallas kernels for 0%

profile of v1, /device:TPU:0, one launch (start us, length us, event | category | flops | bytes accessed | tf_op | source)
XLA Modules:
  0.0 1275.4 jit_solution(8196220181000438740)
XLA Ops:
  9.4 1.3 fusion.63
  10.7 26.0 %all-gather.10.cloned.1.call-done = bf16[1152,512]{1,0:T(8,128)(2,1)} async-done(((bf16[144,512]{1,0:T(8,128)(2,1)}), bf16[1152,512]{1,0:T(8,128)(2,1)}) %all-gather.10.cloned.1.call-update) | async-done | bytes 1179664 | tf_op jit(solution)/shard_map/all_gather | solution.py:92
  36.7 2.0 fusion.78
  39.7 1.8 fusion.72
  44.8 22.8 %all-gather.14.cloned.1.call-done = bf16[1152,1024]{1,0:T(8,128)(2,1)} async-done(((bf16[144,1024]{1,0:T(8,128)(2,1)}), bf16[1152,1024]{1,0:T(8,128)(2,1)}) %all-gather.14.cloned.1.call-update) | async-done | bytes 2359312 | tf_op jit(solution)/shard_map/all_gather | solution.py:91
  67.6 3.1 copy.39
  70.8 1.0 multiply_reduce_fusion.11
  73.0 25.0 %all-gather.12.cloned.1.call-done = bf16[2048,512]{1,0:T(8,128)(2,1)} async-done(((bf16[256,512]{1,0:T(8,128)(2,1)}), bf16[2048,512]{1,0:T(8,128)(2,1)}) %all-gather.12.cloned.1.call-update) | async-done | bytes 2097168 | tf_op jit(solution)/shard_map/all_gather | solution.py:109
  98.0 2.9 while.37
  98.6 1.6 fusion.144
  100.2 0.7 select_reduce_fusion.2
  101.0 2.8 while.38
  101.6 2.2 fusion.148
  104.8 24.0 %all-gather.16.cloned.1.call-done = bf16[1024,1152]{1,0:T(8,128)(2,1)} async-done(((bf16[128,1152]{1,0:T(8,128)(2,1)}), bf16[1024,1152]{1,0:T(8,128)(2,1)}) %all-gather.16.cloned.1.call-update) | async-done | bytes 2359312 | tf_op jit(solution)/shard_map/all_gather | solution.py:93
  128.8 2.7 multiply_reduce_fusion.7
  132.4 84.5 %all-gather.18.cloned.1.call-done = bf16[1152,6912]{0,1:T(8,128)(2,1)} async-done(((bf16[1152,864]{0,1:T(8,128)(2,1)}), bf16[1152,6912]{0,1:T(8,128)(2,1)}) %all-gather.18.cloned.1.call-update) | async-done | bytes 15925264 | tf_op jit(solution)/shard_map/all_gather | solution.py:94
  216.9 16.5 %fusion.84 = f32[256,6912]{1,0:T(8,128)} fusion(bf16[256,1152]{1,0:T(8,128)(2,1)S(1)} %multiply_convert_fusion.4, bf16[1152,6912]{0,1:T(8,128)(2,1)} %all-gather.18.cloned.1.call-done), kind=kOutput, calls=%fused_computation.160 | convolution fusion | flops 4076863488 | bytes 23592960 | tf_op jit(solution)/shard_map/dot_general | solution.py:167
  233.4 71.5 %all-gather.20.cloned.1.call-done = bf16[1152,6912]{0,1:T(8,128)(2,1)} async-done(((bf16[1152,864]{0,1:T(8,128)(2,1)}), bf16[1152,6912]{0,1:T(8,128)(2,1)}) %all-gather.20.cloned.1.call-update) | async-done | bytes 15925264 | tf_op jit(solution)/shard_map/all_gather | solution.py:95
  304.9 12.7 multiply_convert_fusion.1
  317.6 75.5 %all-gather.22.cloned.1.call-done = bf16[6912,1152]{1,0:T(8,128)(2,1)} async-done(((bf16[864,1152]{1,0:T(8,128)(2,1)}), bf16[6912,1152]{1,0:T(8,128)(2,1)}) %all-gather.22.cloned.1.call-update) | async-done | bytes 15925264 | tf_op jit(solution)/shard_map/all_gather | solution.py:96
  393.1 10.5 multiply_reduce_fusion.5
  404.0 1.2 multiply_convert_fusion.3
  405.2 16.0 %multiply_convert_fusion = (bf16[256,6912]{1,0:T(8,128)(2,1)}, bf16[256,6912]{1,0:T(8,128)(2,1)}) fusion(f32[256,6912]{1,0:T(8,128)} %fusion.84, f32[256,6912]{1,0:T(8,128)} %get-tuple-element.377, bf16[256,1152]{1,0:T(8,128)(2,1)S(1)} %get-tuple-element.358, bf16[6912,1152]{1,0:T(8,128)(2,1)} %all-gather.22.cloned.1.call-done), kind=kOutput, calls=%fused_computation.60 | convolution fusion | flops 4119330816 | bytes 37748736 | tf_op jit(solution)/shard_map/dot_general | solution.py:49
  421.3 10.5 fusion.85
  431.8 9.5 multiply_reduce_fusion
  441.4 0.8 multiply_reduce_fusion.1
  443.1 0.8 copy-done.24
  444.4 0.9 convolution_convert_fusion.6
  445.9 1.1 broadcast.270
  446.9 1.5 broadcast_in_dim.41.clone
  448.4 7.5 while.39
  448.9 1.7 bitcast_select_fusion.4
  450.7 1.5 fusion.159
  452.2 1.6 fusion.160
  455.1 0.8 constant_dynamic-update-slice_fusion.2
  456.2 0.9 copy-done.2
  460.3 2.3 convolution_convert_fusion.4
  462.7 2.3 convolution_convert_fusion.3
  465.0 47.4 %reduce-scatter.8.cloned.1.call-done = bf16[256,512]{1,0:T(8,128)(2,1)} async-done(((bf16[2048,512]{1,0:T(8,128)(2,1)}), bf16[256,512]{1,0:T(8,128)(2,1)}) %reduce-scatter.8.cloned.1.call-update) | async-done | bytes 262160 | tf_op jit(solution)/shard_map/reduce_scatter | solution.py:223
  512.4 0.9 slice.80
  513.4 1.0 convert_element_type.217
  515.3 1.6 convolution_convert_fusion.5
  517.0 11.0 convolution_convert_fusion.2
  528.1 10.9 convolution_convert_fusion.1
  539.1 1.0 copy-done.22
  540.1 10.9 convolution_convert_fusion
  551.1 7.6 reduce-scatter.10.cloned.1.call-done
  559.0 45.4 %reduce-scatter.14.cloned.1.call-done = bf16[128,1152]{1,0:T(8,128)(2,1)} async-done(((bf16[1024,1152]{1,0:T(8,128)(2,1)}), bf16[128,1152]{1,0:T(8,128)(2,1)}) %reduce-scatter.14.cloned.1.call-update) | async-done | bytes 294928 | tf_op jit(solution)/shard_map/reduce_scatter | solution.py:262
  604.4 40.4 %reduce-scatter.12.cloned.1.call-done = bf16[144,512]{1,0:T(8,128)(2,1)} async-done(((bf16[1152,512]{1,0:T(8,128)(2,1)}), bf16[144,512]{1,0:T(8,128)(2,1)}) %reduce-scatter.12.cloned.1.call-update) | async-done | bytes 147472 | tf_op jit(solution)/shard_map/reduce_scatter | solution.py:259
  644.7 116.4 %reduce-scatter.16.cloned.1.call-done = bf16[1152,864]{0,1:T(8,128)(2,1)} async-done(((bf16[1152,6912]{0,1:T(8,128)(2,1)}), bf16[1152,864]{0,1:T(8,128)(2,1)}) %reduce-scatter.16.cloned.1.call-update) | async-done | bytes 1990672 | tf_op jit(solution)/shard_map/reduce_scatter | solution.py:265
  761.1 116.9 %reduce-scatter.18.cloned.1.call-done = bf16[1152,864]{0,1:T(8,128)(2,1)} async-done(((bf16[1152,6912]{0,1:T(8,128)(2,1)}), bf16[1152,864]{0,1:T(8,128)(2,1)}) %reduce-scatter.18.cloned.1.call-update) | async-done | bytes 1990672 | tf_op jit(solution)/shard_map/reduce_scatter | solution.py:268
  878.1 116.4 %reduce-scatter.20.cloned.1.call-done = bf16[864,1152]{1,0:T(8,128)(2,1)} async-done(((bf16[6912,1152]{1,0:T(8,128)(2,1)}), bf16[864,1152]{1,0:T(8,128)(2,1)}) %reduce-scatter.20.cloned.1.call-update) | async-done | bytes 1990672 | tf_op jit(solution)/shard_map/reduce_scatter | solution.py:271
  997.5 3.0 fusion.62
  1000.5 24.3 %all-reduce.6 = (bf16[1152]{0:T(1024)(128)(2,1)S(1)}, bf16[1152]{0:T(1024)(128)(2,1)S(1)}, bf16[1152]{0:T(1024)(128)(2,1)S(1)}, bf16[1152]{0:T(1024)(128)(2,1)S(...) all-reduce(bf16[1152]{0:T(1024)(128)(2,1)S(1)} %get-tuple-element.2, ...), channel_id=10, replica_groups=mesh['dp'=4,'seq'=8] {'seq'}, use_global_device_ids=true, to_apply=%region_35.36.clone | all-reduce | flops 5120 | bytes 20480
  1025.2 11.8 all-reduce.7
  1040.3 1.3 fusion.61
  1041.7 1.5 reduce_sum.205
  1043.2 0.9 convert_element_type.219
  1044.0 212.6 %all-reduce.11.cloned.1.call-done = (bf16[144,512]{1,0:T(8,128)(2,1)}, bf16[128,1152]{1,0:T(8,128)(2,1)}, bf16[1152,864]{0,1:T(8,128)(2,1)}, bf16[1152,864]{0,1:T(8,128)(2,1)}, bf16[864,1152]{1,0:T(8,128)(2,1)}) async-done(((bf16[144,512]{1,0:T(8,128)(2,1)}, bf16[128,1152]{1,0:T(8,128)(2,1)}, bf16[1152,864]{0,1:T(8,128)(2,1)}, bf16[1152,864]{0,1:T(8,128)(2,1)}, bf16[864,1152]{1,0:T(8,128)(2,1)}), ...) | async-done | bytes 6414352 | tf_op jit(solution)/shard_map/psum | solution.py:295
  1256.7 1.7 convert_element_type.221
  1258.3 1.8 convert_element_type.223
  1260.2 3.9 convert_element_type.225
  1264.0 2.2 convert_element_type.227
  1266.4 2.2 convert_element_type.229
  (213 shorter events, 25.2 us)
Async XLA Ops:
  7.2 32.4 %copy-start.42 = (f32[256]{0:T(256)S(1)}, f32[256]{0:T(256)}, u32[]{:S(2)}) copy-start(f32[256]{0:T(256)} %param.36) | copy-start | bytes 3076
  7.2 29.5 %all-gather.10.cloned.1.call-start = ((), (), s32[]{:S(2)}) async-start(), calls=%async_computation.7 | async-start | bytes 1327104 | tf_op jit(solution)/shard_map/all_gather | solution.py:92
  7.9 59.7 %all-gather.14.cloned.1.call-start = ((), (), s32[]{:S(2)}) async-start(), calls=%async_computation.9 | async-start | bytes 2654208 | tf_op jit(solution)/shard_map/all_gather | solution.py:91
  8.7 89.4 %all-gather.12.cloned.1.call-start = ((), (), s32[]{:S(2)}) async-start(), calls=%async_computation.8 | async-start | bytes 2359296 | tf_op jit(solution)/shard_map/all_gather | solution.py:109
  9.4 30.3 %copy-start.44 = (f32[1,256]{1,0:T(1,128)}, f32[1,256]{1,0:T(1,128)S(1)}, u32[]{:S(2)}) copy-start(f32[1,256]{1,0:T(1,128)S(1)} %convert_element_type.197) | copy-start | bytes 3076
  9.4 32.0 %copy-start.46 = (f32[128]{0:T(128)}, f32[128]{0:T(128)S(1)}, u32[]{:S(2)}) copy-start(f32[128]{0:T(128)S(1)} %negate_power_fusion) | copy-start | bytes 1540
  10.7 60.0 %copy-start.37 = (f32[256]{0:T(256)}, f32[256]{0:T(256)S(1)}, u32[]{:S(2)}) copy-start(f32[256]{0:T(256)S(1)} %add_rsqrt_fusion.5) | copy-start | bytes 3076
  38.7 0.8 copy-start.19
  39.5 1.9 copy-start.39
  42.2 86.6 %all-gather.16.cloned.1.call-start = ((), (), s32[]{:S(2)}) async-start(), calls=%async_computation.10 | async-start | bytes 2654208 | tf_op jit(solution)/shard_map/all_gather | solution.py:93
  42.8 174.1 %all-gather.18.cloned.1.call-start = ((), (), s32[]{:S(2)}) async-start(), calls=%async_computation.11 | async-start | bytes 17915904 | tf_op jit(solution)/shard_map/all_gather | solution.py:94
  43.4 1.4 copy-start.31
  43.4 261.5 %all-gather.20.cloned.1.call-start = ((), (), s32[]{:S(2)}) async-start(), calls=%async_computation.12 | async-start | bytes 17915904 | tf_op jit(solution)/shard_map/all_gather | solution.py:95
  44.0 349.1 %all-gather.22.cloned.1.call-start = ((), (), s32[]{:S(2)}) async-start(), calls=%async_computation.13 | async-start | bytes 17915904 | tf_op jit(solution)/shard_map/all_gather | solution.py:96
  44.7 467.7 %reduce-scatter.8.cloned.1.call-start = ((), (), s32[]{:S(2)}) async-start(), calls=%async_computation.14 | async-start | bytes 2359296 | tf_op jit(solution)/shard_map/reduce_scatter | solution.py:223
  67.6 3.1 copy-start.3
  67.6 3.1 copy-start.33
  70.7 1.0 copy-start.41
  71.8 1.0 copy-start.10
  103.9 1.0 copy-start.12
  104.8 26.7 %copy-start.16 = (bf16[256,1024]{1,0:T(8,128)(2,1)}, bf16[256,1024]{1,0:T(8,128)(2,1)S(1)}, u32[]{:S(2)}) copy-start(bf16[256,1024]{1,0:T(8,128)(2,1)S(1)} %convert_element_type.204) | copy-start | bytes 1572868
  104.8 26.7 %copy-start.32 = (f32[1152]{0:T(1024)S(1)}, f32[1152]{0:T(1024)}, u32[]{:S(2)}) copy-start(f32[1152]{0:T(1024)} %param.32) | copy-start | bytes 13828
  128.8 2.7 copy-start.4
  131.5 0.7 copy-start.36
  132.4 172.5 %copy-start.14 = (bf16[256,1152]{1,0:T(8,128)(2,1)}, bf16[256,1152]{1,0:T(8,128)(2,1)S(1)}, u32[]{:S(2)}) copy-start(bf16[256,1152]{1,0:T(8,128)(2,1)S(1)} %multiply_convert_fusion.4) | copy-start | bytes 1769476
  393.1 10.5 copy-start.8
  393.1 10.5 copy-start.35
  405.2 16.1 %copy-start.21 = (bf16[256,1152]{1,0:T(8,128)(2,1)}, bf16[256,1152]{1,0:T(8,128)(2,1)S(1)}, u32[]{:S(2)}) copy-start(bf16[256,1152]{1,0:T(8,128)(2,1)S(1)} %get-tuple-element.358) | copy-start | bytes 1769476
  421.3 10.5 copy-start.18
  431.8 9.5 copy-start.9
  442.1 1.0 copy-start.6
  442.1 2.3 copy-start.23
  443.1 0.8 copy-start.24
  444.4 1.2 copy-start.13
  450.7 1.5 copy-start
  453.8 1.0 copy-start.1
  455.9 1.2 copy-start.2
  456.0 102.7 %reduce-scatter.10.cloned.1.call-start = ((), (), s32[]{:S(2)}) async-start(), calls=%async_computation.15 | async-start | bytes 2654208 | tf_op jit(solution)/shard_map/reduce_scatter | solution.py:256
  457.2 0.9 copy-start.29
  457.2 1.0 copy-start.30
  457.5 1.3 copy-start.11
  459.2 1.1 copy-start.5
  459.2 1.1 copy-start.34
  459.2 1.1 copy-start.38
  460.3 2.4 copy-start.17
  460.3 2.4 copy-start.25
  462.6 141.8 %reduce-scatter.14.cloned.1.call-start = ((), (), s32[]{:S(2)}) async-start(), calls=%async_computation.17 | async-start | bytes 2654208 | tf_op jit(solution)/shard_map/reduce_scatter | solution.py:262
  464.9 49.4 %copy-start.45 = (f32[1,256]{1,0:T(1,128)S(1)}, f32[1,256]{1,0:T(1,128)}, u32[]{:S(2)}) copy-start(f32[1,256]{1,0:T(1,128)} %copy-done.44) | copy-start | bytes 3076
  464.9 49.4 %copy-start.47 = (f32[128]{0:T(128)S(1)}, f32[128]{0:T(128)}, u32[]{:S(2)}) copy-start(f32[128]{0:T(128)} %copy-done.46) | copy-start | bytes 1540
  464.9 50.0 %copy-start.20 = (f32[256,512]{1,0:T(8,128)S(1)}, f32[256,512]{1,0:T(8,128)}, u32[]{:S(2)}) copy-start(f32[256,512]{1,0:T(8,128)} %copy-done.19) | copy-start | bytes 1572868
  464.9 50.0 %copy-start.40 = (f32[256]{0:T(256)S(1)}, f32[256]{0:T(256)}, u32[]{:S(2)}) copy-start(f32[256]{0:T(256)} %copy-done.39) | copy-start | bytes 3076
  464.9 50.0 %copy-start.43 = (f32[256]{0:T(256)S(1)}, f32[256]{0:T(256)}, u32[]{:S(2)}) copy-start(f32[256]{0:T(256)} %param.36) | copy-start | bytes 3076
  465.0 179.8 %reduce-scatter.12.cloned.1.call-start = ((), (), s32[]{:S(2)}) async-start(), calls=%async_computation.16 | async-start | bytes 1327104 | tf_op jit(solution)/shard_map/reduce_scatter | solution.py:259
  515.2 1.9 copy-start.15
  517.0 244.2 %reduce-scatter.16.cloned.1.call-start = ((), (), s32[]{:S(2)}) async-start(), calls=%async_computation.18 | async-start | bytes 17915904 | tf_op jit(solution)/shard_map/reduce_scatter | solution.py:265
  528.1 350.0 %reduce-scatter.18.cloned.1.call-start = ((), (), s32[]{:S(2)}) async-start(), calls=%async_computation.19 | async-start | bytes 17915904 | tf_op jit(solution)/shard_map/reduce_scatter | solution.py:268
  539.0 1.1 copy-start.22
  539.1 455.4 %reduce-scatter.20.cloned.1.call-start = ((), (), s32[]{:S(2)}) async-start(), calls=%async_computation.20 | async-start | bytes 17915904 | tf_op jit(solution)/shard_map/reduce_scatter | solution.py:271
  551.0 490.6 %all-gather.24.cloned.1.call-start = ((), (), s32[]{:S(2)}) async-start(), calls=%async_computation.21 | async-start | bytes 1474560 | tf_op jit(solution)/shard_map/all_gather | solution.py:13
  558.7 698.0 %all-reduce.11.cloned.1.call-start = ((), (), s32[]{:S(2)}) async-start(), calls=%async_computation.22 | async-start | bytes 12828672 | tf_op jit(solution)/shard_map/psum | solution.py:295
  994.4 2.5 copy-start.28
  997.5 42.8 %copy-start.7 = (f32[256,1152]{1,0:T(8,128)S(1)}, f32[256,1152]{1,0:T(8,128)}, u32[]{:S(2)}) copy-start(f32[256,1152]{1,0:T(8,128)} %copy-done.6) | copy-start | bytes 3538948
  1260.1 3.9 copy-start.27
  1264.0 2.4 copy-start.26
  (1 other events, 0.7 us)
Sparse Core Ops, SparseCore 0:
  9.9 26.7 all-gather.9
  38.6 29.0 all-gather.13
  70.1 27.8 all-gather.11
  99.8 29.0 all-gather.15
  130.6 86.2 all-gather.17
  218.6 86.2 all-gather.19
  306.8 86.2 all-gather.21
  456.1 56.3 reduce-scatter.7
  516.2 42.4 reduce-scatter.9
  561.9 42.4 reduce-scatter.13
  608.0 36.7 reduce-scatter.11
  648.2 112.8 reduce-scatter.15
  765.2 112.8 reduce-scatter.17
  881.6 112.8 reduce-scatter.19
  995.9 30.4 all-gather.23
  1029.3 227.3 all-reduce.10
